TPU v7x, 256 devices: a whole 4x4x8 slice. The times are simulated.
256 devices in a mesh: ctx: 16 (over x, z_lo), sec: 8 (over y, core), dp: 2 (over z_hi).
Axes of the slice: x: 4, y: 4, z: 8 (z_hi: 2, z_lo: 4; z = z_hi * 4 + z_lo), core: 2. Of those that a mesh axis runs over, the one named last changes fastest.
Arguments:
- fresh_input: bfloat16 [2, 4096, 1536], P('dp', 'ctx'), may hold values from -6 to 6
- carried: bfloat16 [8, 2, 4096, 1536], P('sec', 'dp', 'ctx'), may hold values from -6 to 6
- qkv_weight: bfloat16 [8, 1536, 4608], P('sec', ('ctx', 'dp')), as said below
- out_weight: bfloat16 [8, 1536, 1536], P('sec', ('ctx', 'dp')), may hold values from -0.15625 to 0.15625
- rate_weight: bfloat16 [8, 1536, 6], P('sec', ('ctx', 'dp')), may hold values from -0.15625 to 0.15625
- fast_state: float32 [8, 2, 3, 6, 768, 256], P('sec', 'dp', None, None, 'ctx'), may hold values from -6 to 6
Outputs:
- passed: bfloat16 [8, 2, 4096, 1536], P('sec', 'dp', 'ctx')
- new_state: float32 [8, 2, 3, 6, 768, 256], P('sec', 'dp', None, None, 'ctx')
Inputs may be any that keep to these rules, and one draw needn't show every extreme that they name: Every entry of qkv_weight is at most 6 / sqrt(1536) in magnitude.
All inputs are finite; a program needn't handle non-finite values.
Results may differ from a plain program's by a relative error of at most 0.022.
Values may be sent and summed in bfloat16 or wider, within the bound.
No kernel may reach another device: no remote copies, remote signals or barrier semaphores. Data moves between devices by JAX's collectives and lax.ppermute only.
A program may use at most 128 MiB of HBM per device.

v0:
```python
import jax
import jax.numpy as jnp
from jax import lax
from jax.sharding import Mesh
from jax.sharding import PartitionSpec as P

NS_STEPS = 2
CTX = ("ctx_0", "ctx_1")
CTX_DP = ("ctx_0", "ctx_1", "dp")


linear_coef = 3.4445
cubic_coef = -4.775
quintic_coef = 2.0315
update_scale = 8.0
highest = lax.Precision.HIGHEST


def from_behind(block, axis, distance):
    devices = range(lax.axis_size(axis))
    route = [(i - distance, i) for i in devices if i - distance in devices]
    return lax.ppermute(block, axis, route)


def side_by_side(arrays, axis, dim, along):
    ends, at = ([], 0)
    for a in arrays[:-1]:
        at += a.shape[along]
        ends.append(at)
    both = jnp.concatenate(arrays, axis=along)
    return tuple(jnp.split(lax.all_gather(both, axis, axis=dim, tiled=True), ends, axis=along))


def sum_by_axis(shard, axes, dim):
    if not axes:
        return shard
    nearer = lax.psum_scatter(shard, axes[0], scatter_dimension=dim, tiled=True)
    return sum_by_axis(nearer, axes[1:], dim)


def swish(values):
    return values * jax.nn.sigmoid(values)


def unit_rows(values):
    return values / jnp.sqrt(jnp.sum(values * values, axis=-1, keepdims=True) + 1e-06)


def gram_local(current):
    return jnp.einsum("mhrd,mhre->mhde", current, current, precision=highest)


def local(fresh_input, carried, qkv_weight, out_weight, rate_weight, fast_state):
    received = from_behind(carried, "sec", 1)
    is_first = lax.axis_index("sec") == 0
    inputs = jnp.where(is_first, fresh_input[None], received)[0, 0]
    count = inputs.shape[0]
    heads = rate_weight.shape[2]
    head_dim = fast_state.shape[5]
    previous = fast_state[0, 0]
    gathered = lax.all_gather(previous.astype(jnp.bfloat16), CTX, axis=2, tiled=True)
    full_qkv, full_out, full_rate = side_by_side(
        (qkv_weight[0], out_weight[0], rate_weight[0]), CTX_DP, 0, 1
    )
    projected = jnp.dot(inputs, full_qkv, preferred_element_type=jnp.float32)
    rate_pre = jnp.dot(inputs, full_rate, preferred_element_type=jnp.float32)
    projected = projected.reshape(count, 3, heads, head_dim)
    query_rows = unit_rows(swish(projected[:, 0])).astype(jnp.bfloat16)
    key_rows = unit_rows(swish(projected[:, 1])).astype(jnp.bfloat16)
    value_rows = projected[:, 2].astype(jnp.bfloat16)
    rates = jax.nn.softplus(rate_pre)
    gate_fast, up_fast, down_fast = (gathered[0], gathered[1], gathered[2])
    gate_query = jnp.einsum(
        "thd,hfd->thf", query_rows, gate_fast, preferred_element_type=jnp.float32
    )
    up_query = jnp.einsum("thd,hfd->thf", query_rows, up_fast, preferred_element_type=jnp.float32)
    hidden = (swish(gate_query) * up_query).astype(jnp.bfloat16)
    mixture = jnp.einsum("thf,hfd->thd", hidden, down_fast, preferred_element_type=jnp.float32)
    head_out = (
        mixture * lax.rsqrt(jnp.mean(mixture * mixture, axis=-1, keepdims=True) + 1e-05)
    ).astype(jnp.bfloat16)
    head_out = head_out.reshape(count, heads * head_dim)
    branch_out = jnp.dot(head_out, full_out, preferred_element_type=jnp.float32)
    passed = (inputs.astype(jnp.float32) + branch_out).astype(jnp.bfloat16)
    gate_pre = jnp.einsum("thd,hfd->thf", key_rows, gate_fast, preferred_element_type=jnp.float32)
    up_pre = jnp.einsum("thd,hfd->thf", key_rows, up_fast, preferred_element_type=jnp.float32)
    sigma = jax.nn.sigmoid(gate_pre)
    gate_act = gate_pre * sigma
    key_hidden = (gate_act * up_pre).astype(jnp.bfloat16)
    scaled_values = (rates[:, :, None] * value_rows.astype(jnp.float32)).astype(jnp.bfloat16)
    hidden_grad = -jnp.einsum(
        "thd,hfd->thf", scaled_values, down_fast, preferred_element_type=jnp.float32
    )
    up_grad = (hidden_grad * gate_act).astype(jnp.bfloat16)
    gate_grad = (hidden_grad * up_pre * sigma * (1.0 + gate_pre * (1.0 - sigma))).astype(
        jnp.bfloat16
    )
    grad_gate = jnp.einsum("thf,thd->hfd", gate_grad, key_rows, preferred_element_type=jnp.float32)
    grad_up = jnp.einsum("thf,thd->hfd", up_grad, key_rows, preferred_element_type=jnp.float32)
    grad_down = -jnp.einsum(
        "thf,thd->hfd", key_hidden, scaled_values, preferred_element_type=jnp.float32
    )
    partial_value = jnp.stack([grad_gate, grad_up, grad_down])
    gradient = sum_by_axis(partial_value.astype(jnp.bfloat16), CTX, 2).astype(jnp.float32)
    current = gradient
    for iteration in range(NS_STEPS):
        square = lax.psum(gram_local(current).astype(jnp.bfloat16), CTX).astype(jnp.float32)
        if iteration == 0:
            inverse_norm = lax.rsqrt(jnp.trace(square, axis1=-2, axis2=-1) + 1e-06)[
                :, :, None, None
            ]
            current = current * inverse_norm
            square = square * inverse_norm * inverse_norm
        product = jnp.einsum("mhrd,mhde->mhre", current, square, precision=highest)
        current = (
            linear_coef * current
            + cubic_coef * product
            + quintic_coef * jnp.einsum("mhrd,mhde->mhre", product, square, precision=highest)
        )
    stepped = previous - update_scale * current
    rescale = jnp.sqrt(jnp.mean(previous * previous, axis=-1, keepdims=True) + 1e-06) * lax.rsqrt(
        jnp.mean(stepped * stepped, axis=-1, keepdims=True) + 1e-06
    )
    new_state = (stepped * rescale)[None, None]
    return (passed[None, None], new_state)


def solution(mesh):
    split = Mesh(
        mesh.devices.reshape(4, 4, mesh.shape["sec"], mesh.shape["dp"]),
        ("ctx_0", "ctx_1", "sec", "dp"),
    )
    in_specs = (
        P("dp", CTX, None),
        P("sec", "dp", CTX, None),
        P("sec", CTX_DP, None),
        P("sec", CTX_DP, None),
        P("sec", CTX_DP, None),
        P("sec", "dp", None, None, CTX, None),
    )
    out_specs = (P("sec", "dp", CTX, None), P("sec", "dp", None, None, CTX, None))
    return jax.shard_map(local, mesh=split, in_specs=in_specs, out_specs=out_specs, check_vma=False)
```

profile of v0, /device:TPU:1, one launch (start us, length us, event | category | flops | bytes accessed | tf_op | source)
XLA Modules:
  0.0 1719.5 jit_solution(13796649520828619876)
XLA Ops:
  7.2 0.0 all-gather.3.cloned.1.call-start
  7.2 0.9 copy.8
  8.2 2.0 pad_maximum_fusion.1
  10.2 0.0 all-gather.5.cloned.1.call-start
  10.2 0.8 bitcast_convert_fusion
  11.0 0.0 all-gather.5.cloned.1.call-update
  11.0 0.0 reduce-scatter.3.cloned.1.call-start
  11.1 4.6 collective-permute-start
  15.7 8.9 collective-permute-done
  24.6 0.1 bitcast_select_fusion
  24.7 1004.5 %all-gather.3.cloned.1.call-done = bf16[1536,6150]{1,0:T(8,128)(2,1)} async-done(((bf16[48,6150]{1,0:T(8,128)(2,1)}), bf16[1536,6150]{1,0:T(8,128)(2,1)}) %all-gather.3.cloned.1.call-update) | async-done | bytes 18892816 | tf_op jit(solution)/shard_map/all_gather | solution.py:31
  1029.2 12.6 slice_bitcast_fusion
  1041.9 18.7 %copy.9 = bf16[4608,1536]{1,0:T(8,128)(2,1)} copy(bf16[4608,1536]{0,1:T(8,128)(2,1)} %slice_bitcast_fusion) | data formatting | bytes 28311552 | tf_op jit(solution)/shard_map/dot_general | solution.py:65
  1060.5 7.5 fusion.59
  1068.0 2.2 copy-done.2
  1070.3 1.0 multiply_reduce_fusion
  1071.3 1.4 compare_select_fusion
  1072.7 119.2 %all-gather.5.cloned.1.call-done = bf16[3,6,768,256]{3,2,1,0:T(8,128)(2,1)} async-done(((bf16[3,6,48,256]{3,2,1,0:T(8,128)(2,1)}), bf16[3,6,768,256]{3,2,1,0:T(8,128)(2,1)}) %all-gather.5.cloned.1.call-update) | async-done | bytes 7077904 | tf_op jit(solution)/shard_map/all_gather | solution.py:61
  1191.9 5.7 fusion.34
  1197.5 1.5 copy-done.7
  1199.0 0.9 fusion.37
  1199.9 5.9 convert_bitcast_fusion
  1205.9 3.1 fusion.36
  1209.0 7.9 convert_bitcast_fusion.1
  1216.9 5.7 fusion.21
  1222.6 3.5 pad_maximum_fusion
  1226.1 0.0 reduce-scatter.3.cloned.1.call-update
  1226.1 0.0 reduce-scatter.5.cloned.1.call-start
  1226.2 71.1 %reduce-scatter.3.cloned.1.call-done = bf16[3,6,192,256]{3,2,1,0:T(8,128)(2,1)} async-done(((bf16[3,6,768,256]{3,2,1,0:T(8,128)(2,1)}), bf16[3,6,192,256]{3,2,1,0:T(8,128)(2,1)}) %reduce-scatter.3.cloned.1.call-update) | async-done | bytes 1769488 | tf_op jit(solution)/shard_map/reduce_scatter | solution.py:37
  1297.3 0.0 all-reduce.3.cloned.1.call-start
  1297.3 45.6 %reduce-scatter.5.cloned.1.call-done = bf16[3,6,48,256]{3,2,1,0:T(8,128)(2,1)} async-done(((bf16[3,6,192,256]{3,2,1,0:T(8,128)(2,1)}), bf16[3,6,48,256]{3,2,1,0:T(8,128)(2,1)}) %reduce-scatter.5.cloned.1.call-update) | async-done | bytes 442384 | tf_op jit(solution)/shard_map/reduce_scatter | solution.py:37
  1342.9 3.4 convolution_convert_fusion.1
  1346.3 0.0 all-reduce.3.cloned.1.call-update
  1346.3 0.3 all-reduce.5.cloned.1.call-start
  1346.6 0.2 fusion.56
  1346.8 5.3 fusion.35
  1352.2 162.4 %all-reduce.3.cloned.1.call-done = bf16[3,6,256,256]{3,2,1,0:T(8,128)(2,1)} async-done(((bf16[3,6,256,256]{3,2,1,0:T(8,128)(2,1)}), bf16[3,6,256,256]{3,2,1,0:T(8,128)(2,1)}) %all-reduce.3.cloned.1.call-update) | async-done | bytes 2359312 | tf_op jit(solution)/shard_map/psum | solution.py:107
  1514.5 2.5 fusion
  1517.1 3.5 fusion.4
  1520.6 3.5 fusion.50
  1524.1 5.5 convolution_convert_fusion
  1529.6 7.9 fusion.45
  1537.5 1.5 fusion.46
  1539.0 4.6 fusion.57
  1543.7 163.1 %all-reduce.5.cloned.1.call-done = bf16[3,6,256,256]{3,2,1,0:T(8,128)(2,1)} async-done(((bf16[3,6,256,256]{3,2,1,0:T(8,128)(2,1)}), bf16[3,6,256,256]{3,2,1,0:T(8,128)(2,1)}) %all-reduce.5.cloned.1.call-update) | async-done | bytes 2359312 | tf_op jit(solution)/shard_map/psum | solution.py:107
  1706.7 3.2 fusion.77
  1709.9 1.6 multiply_reduce_fusion.2
  1711.6 1.1 multiply_bitcast_fusion
  (31 shorter events, 0.2 us)
Async XLA Ops:
  7.2 3.0 copy-start.1
  7.2 3.9 copy-start.9
  7.2 17.4 %copy-start.8 = (bf16[1,256,1536]{2,1,0:T(8,128)(2,1)S(1)}, bf16[1,256,1536]{2,1,0:T(8,128)(2,1)}, u32[]{:S(2)}) copy-start(bf16[1,256,1536]{2,1,0:T(8,128)(2,1)} %param.6) | copy-start | bytes 2359300
  7.2 1022.0 %all-gather.3.cloned.1.call-start = ((), (), s32[]{:S(2)}) async-start(), calls=%async_computation.2 | async-start | bytes 19869696 | tf_op jit(solution)/shard_map/all_gather | solution.py:31
  10.2 1181.7 %all-gather.5.cloned.1.call-start = ((), (), s32[]{:S(2)}) async-start(), calls=%async_computation.3 | async-start | bytes 7520256 | tf_op jit(solution)/shard_map/all_gather | solution.py:61
  11.0 1286.2 %reduce-scatter.3.cloned.1.call-start = ((), (), s32[]{:S(2)}) async-start(), calls=%async_computation.4 | async-start | bytes 8847360 | tf_op jit(solution)/shard_map/reduce_scatter | solution.py:37
  11.1 13.5 collective-permute-start
  1068.0 2.2 copy-start.2
  1071.3 126.3 %slice-start = ((s8[4718592]{0:T(1024)(128)(4,1)}), s8[524288]{0:T(1024)(128)(4,1)S(1)}, s32[]{:S(2)}) async-start(s8[4718592]{0:T(1024)(128)(4,1)} %bitcast.183), calls=%async_computation.8 | async-start | bytes 1048576
  1191.9 5.7 slice-start.1
  1191.9 7.2 copy-start.7
  1216.9 5.7 copy-start.3
  1216.9 5.7 copy-start.4
  1226.1 116.8 %reduce-scatter.5.cloned.1.call-start = ((), (), s32[]{:S(2)}) async-start(), calls=%async_computation.5 | async-start | bytes 2211840 | tf_op jit(solution)/shard_map/reduce_scatter | solution.py:37
  1297.3 217.3 %all-reduce.3.cloned.1.call-start = ((), (), s32[]{:S(2)}) async-start(), calls=%async_computation.6 | async-start | bytes 4718592 | tf_op jit(solution)/shard_map/psum | solution.py:107
  1346.3 360.4 %all-reduce.5.cloned.1.call-start = ((), (), s32[]{:S(2)}) async-start(), calls=%async_computation.7 | async-start | bytes 4718592 | tf_op jit(solution)/shard_map/psum | solution.py:107
  1346.8 170.3 %copy-start.6 = (bf16[3,6,48,256]{3,2,1,0:T(8,128)(2,1)S(1)}, bf16[3,6,48,256]{3,2,1,0:T(8,128)(2,1)}, u32[]{:S(2)}) copy-start(bf16[3,6,48,256]{3,2,1,0:T(8,128)(2,1)} %reduce-scatter.5.cloned.1.call-done) | copy-start | bytes 1327108
  1514.5 2.6 copy-start.5
  1706.7 3.2 copy-start
Sparse Core Ops, SparseCore 0:
  10.4 1018.8 all-gather.2
  1031.6 160.2 all-gather.4
  1226.2 70.9 reduce-scatter.2
  1299.7 43.1 reduce-scatter.4
  1346.4 168.0 all-reduce.2
  1529.7 176.9 all-reduce.4
where the time goes:
time: 1730 us; the launch traced here: 1720 us
  waiting for transfers between devices  1570 us (91%)
  matrix products  76.5 us (4%)
  local copies, waits for them, and re-layouts  36 us (2%)
    all_gather x1, waiting for transfers between devices, side_by_side(): lax.all_gather(both, axis, axis=dim, tiled=True)  1000 us
    psum x2, waiting for transfers between devices, local(): lax.psum(gram_local(current).astype(jnp.bfloat16), CTX).astype(jnp.float32)  325 us
    all_gather x1, waiting for transfers between devices, local(): lax.all_gather(previous.astype(jnp.bfloat16), CTX, axis=2, tiled=True)  119 us
    reduce_scatter x2, waiting for transfers between devices, sum_by_axis(): nearer = lax.psum_scatter(shard, axes[0], scatter_dimension=dim, tiled=True)  117 us
  transfers between devices with their start and end apart: 7, of which 7 were waited for; matrix products, arithmetic and copies ran while one was open for 4% of the time, Pallas kernels for 0%

commit v1 on v0

v1 whole, which is shorter than its diff:
```python
import jax
import jax.numpy as jnp
from jax import lax
from jax.sharding import Mesh
from jax.sharding import PartitionSpec as P

CTX = ("xh", "xl", "zl")
CTX_DP = CTX + ("dp",)
LANES = 128

linear_coef = 3.4445
cubic_coef = -4.775
quintic_coef = 2.0315
update_scale = 8.0
highest = lax.Precision.HIGHEST


def swish(values):
    return values * jax.nn.sigmoid(values)


def unit_rows(values):
    return values / jnp.sqrt(jnp.sum(values * values, axis=-1, keepdims=True) + 1e-06)


def swap_pair(block):
    return lax.ppermute(block, "xh", [(0, 1), (1, 0)])


def pair_shard(low, high, is_low, dim):
    kept = jnp.where(is_low, low, high)
    got = swap_pair(jnp.where(is_low, high, low))
    return jnp.concatenate([jnp.where(is_low, kept, got), jnp.where(is_low, got, kept)], axis=dim)


def polynomial(square):
    return (
        linear_coef * jnp.eye(square.shape[-1], dtype=jnp.float32)
        + cubic_coef * square
        + quintic_coef * jnp.einsum("mde,mef->mdf", square, square, precision=highest)
    )


def orthogonalize(gradient):
    square = jnp.einsum("mrd,mre->mde", gradient, gradient, precision=highest)
    inverse_norm = lax.rsqrt(jnp.trace(square, axis1=-2, axis2=-1) + 1e-06)[:, None, None]
    square = square * inverse_norm * inverse_norm
    first = polynomial(square)
    square = jnp.einsum(
        "mde,mef->mdf",
        first,
        jnp.einsum("mde,mef->mdf", square, first, precision=highest),
        precision=highest,
    )
    both = jnp.einsum("mde,mef->mdf", first, polynomial(square), precision=highest)
    return jnp.einsum("mrd,mde->mre", gradient * inverse_norm, both, precision=highest)


def local(fresh_input, carried, qkv_weight, out_weight, rate_weight, fast_state):
    is_low = lax.axis_index("xh") == 0
    sections = lax.axis_size("sec")
    heads = rate_weight.shape[2]
    head_dim = fast_state.shape[5]
    half = heads // 2
    width = half * head_dim
    rows = qkv_weight.shape[1]
    count, channels = fresh_input.shape[1:]

    w = qkv_weight[0].reshape(rows, 3, 2, width)
    rates = jnp.pad(rate_weight[0].reshape(rows, 2, half), ((0, 0), (0, 0), (0, LANES - half)))
    low, high = (
        jnp.concatenate([w[:, 0, h], w[:, 1, h], w[:, 2, h], rates[:, h]], axis=1) for h in (0, 1)
    )
    group_w = lax.all_gather(
        pair_shard(low, high, is_low, 0), ("xl", "zl", "dp"), axis=0, tiled=True
    )
    previous = fast_state[0, 0]
    shard = previous.astype(jnp.bfloat16)
    group_fast = lax.all_gather(
        pair_shard(shard[:, :half], shard[:, half:], is_low, 2), ("xl", "zl"), axis=2, tiled=True
    )
    group_out = lax.all_gather(out_weight[0], ("xl", "zl", "dp"), axis=0, tiled=True)

    is_last = lax.axis_index("sec") == sections - 1
    source = jnp.where(is_last, fresh_input[0], carried[0, 0])
    mine = lax.ppermute(source, "sec", [(i, (i + 1) % sections) for i in range(sections)])
    pairs = [
        (a * sections + i, (1 - a) * sections + (i + 1) % sections)
        for a in (0, 1)
        for i in range(sections)
    ]
    other = lax.ppermute(source, ("xh", "sec"), pairs)
    inputs = jnp.concatenate([mine, other], axis=0)
    ordered = (
        inputs.reshape(2 * count, 2, -1, rows).transpose(0, 2, 1, 3).reshape(2 * count, channels)
    )

    projected = jnp.dot(ordered, group_w, preferred_element_type=jnp.float32)
    part = lambda i: projected[:, i * width : (i + 1) * width].reshape(2 * count, half, head_dim)
    query_rows = unit_rows(swish(part(0))).astype(jnp.bfloat16)
    key_rows = unit_rows(swish(part(1))).astype(jnp.bfloat16)
    value_rows = part(2).astype(jnp.bfloat16)
    rates = jax.nn.softplus(projected[:, 3 * width : 3 * width + half])
    gate_fast, up_fast, down_fast = (group_fast[0], group_fast[1], group_fast[2])

    gate_pre = jnp.einsum("thd,hfd->htf", key_rows, gate_fast, preferred_element_type=jnp.float32)
    up_pre = jnp.einsum("thd,hfd->htf", key_rows, up_fast, preferred_element_type=jnp.float32)
    sigma = jax.nn.sigmoid(gate_pre)
    gate_act = gate_pre * sigma
    key_hidden = (gate_act * up_pre).astype(jnp.bfloat16)
    scaled_values = (rates[:, :, None] * value_rows.astype(jnp.float32)).astype(jnp.bfloat16)
    hidden_grad = -jnp.einsum(
        "thd,hfd->htf", scaled_values, down_fast, preferred_element_type=jnp.float32
    )
    up_grad = (hidden_grad * gate_act).astype(jnp.bfloat16)
    gate_grad = (hidden_grad * up_pre * sigma * (1.0 + gate_pre * (1.0 - sigma))).astype(
        jnp.bfloat16
    )
    grad_gate = jnp.einsum("htf,thd->hfd", gate_grad, key_rows, preferred_element_type=jnp.float32)
    grad_up = jnp.einsum("htf,thd->hfd", up_grad, key_rows, preferred_element_type=jnp.float32)
    grad_down = -jnp.einsum(
        "htf,thd->hfd", key_hidden, scaled_values, preferred_element_type=jnp.float32
    )

    owners = lax.axis_size(("xl", "zl"))
    spread = jnp.concatenate([grad_gate, grad_up, grad_down[: owners - 2 * half]], axis=0)
    shared = lax.psum(grad_down[owners - 2 * half :].astype(jnp.bfloat16), ("xl", "zl"))
    owned = lax.psum_scatter(
        spread.astype(jnp.bfloat16), ("xl", "zl"), scatter_dimension=0, tiled=True
    )
    gradient = jnp.concatenate([owned, shared], axis=0).astype(jnp.float32)
    current = orthogonalize(gradient).astype(jnp.bfloat16)
    shard_rows = previous.shape[2]
    blocks = current.reshape(2, owners, 2, shard_rows, head_dim)
    outgoing = blocks[0].transpose(1, 0, 2, 3).reshape(2 * owners, shard_rows, head_dim)
    arrived = lax.all_to_all(outgoing, CTX, 0, 0, tiled=True)
    arrived = arrived.reshape(2, owners, shard_rows, head_dim)
    mine_last = lax.dynamic_index_in_dim(
        blocks[1], lax.axis_index(("xl", "zl")), 0, keepdims=False
    )
    last = pair_shard(mine_last[0][None], mine_last[1][None], is_low, 0)[:, None]
    current = jnp.concatenate([arrived, last], axis=1).astype(jnp.float32)
    current = current.reshape(2, 3, half, shard_rows, head_dim).transpose(1, 0, 2, 3, 4)
    current = current.reshape(previous.shape)
    stepped = previous - update_scale * current
    rescale = jnp.sqrt(jnp.mean(previous * previous, axis=-1, keepdims=True) + 1e-06) * lax.rsqrt(
        jnp.mean(stepped * stepped, axis=-1, keepdims=True) + 1e-06
    )
    new_state = (stepped * rescale)[None, None]

    gate_query = jnp.einsum(
        "thd,hfd->htf", query_rows, gate_fast, preferred_element_type=jnp.float32
    )
    up_query = jnp.einsum("thd,hfd->htf", query_rows, up_fast, preferred_element_type=jnp.float32)
    hidden = (swish(gate_query) * up_query).astype(jnp.bfloat16)
    mixture = jnp.einsum("htf,hfd->thd", hidden, down_fast, preferred_element_type=jnp.float32)
    head_out = (
        mixture * lax.rsqrt(jnp.mean(mixture * mixture, axis=-1, keepdims=True) + 1e-05)
    ).astype(jnp.bfloat16)
    branch_out = jnp.dot(
        head_out.reshape(2 * count, width), group_out, preferred_element_type=jnp.float32
    )
    from_pair = swap_pair(branch_out[count:].astype(jnp.bfloat16))
    passed = (
        mine.astype(jnp.float32) + (branch_out[:count] + from_pair.astype(jnp.float32))
    ).astype(jnp.bfloat16)
    return (passed[None, None], new_state)


def solution(mesh):
    shape = (2, 2, 4, mesh.shape["sec"], mesh.shape["dp"])
    split = Mesh(mesh.devices.reshape(shape), ("xh", "xl", "zl", "sec", "dp"))
    in_specs = (
        P("dp", CTX, None),
        P("sec", "dp", CTX, None),
        P("sec", CTX_DP, None),
        P("sec", CTX_DP, None),
        P("sec", CTX_DP, None),
        P("sec", "dp", None, None, CTX, None),
    )
    out_specs = (P("sec", "dp", CTX, None), P("sec", "dp", None, None, CTX, None))
    return jax.shard_map(local, mesh=split, in_specs=in_specs, out_specs=out_specs, check_vma=False)
```

time: 1730 us -> 849 us (0.49)
  waiting for transfers between devices: 1570 us -> 728 us
  matrix products: 76.5 us -> 43.6 us
  starting transfers between devices: 5.05 us -> 26.1 us
  local copies, waits for them, and re-layouts: 36 us -> 17.9 us
    all_gather x2 -> x3, waiting for transfers between devices: 1120 us -> 534 us  [the longest x1 358 us: local(): lax.all_gather(pair_shard(low, high, is_low, 0), ('xl', 'zl', 'dp'), axis...]
    psum x2 -> x1, waiting for transfers between devices: 325 us -> 79.8 us  [local(): lax.psum(grad_down[owners - 2 * half:].astype(jnp.bfloat16), ('xl', 'zl'))]
    reduce_scatter x2 -> x1, waiting for transfers between devices: 117 us -> 83.3 us  [local(): lax.psum_scatter(spread.astype(jnp.bfloat16), ('xl', 'zl'), scatter_dimen...]
    dot_general x17, matrix products: 76.5 us -> 43.6 us  [the longest x1 6.82 us: local(): projected = jnp.dot(ordered, group_w, preferred_element_type=jnp.float32)]
    dot_general x2 -> x0, local copies, waits for them, and re-layouts: 31.3 us -> none  [local(): projected = jnp.dot(inputs, full_qkv, preferred_element_type=jnp.float32)]
    ppermute x1 -> x6, starting transfers between devices: 4.58 us -> 22.1 us  [the longest x4 15.1 us: swap_pair(): return lax.ppermute(block, 'xh', [(0, 1), (1, 0)])]
  transfers between devices with their start and end apart: 7 -> 12, of which waited for: 7 -> 9; matrix products, arithmetic and copies ran while one was open for 4% -> 8% of each run, Pallas kernels for 0% -> 0%
where the time goes in v1:
time: 849 us; the launch traced here: 842 us
  waiting for transfers between devices  728 us (86%)
  matrix products  43.6 us (5%)
  starting transfers between devices  26.1 us (3%)
  local copies, waits for them, and re-layouts  17.9 us (2%)
  between operations  14.3 us (2%)
  other arithmetic  12 us (1%)
    all_gather x1, waiting for transfers between devices, local(): lax.all_gather(pair_shard(low, high, is_low, 0), ('xl', 'zl', 'dp'), axis...  358 us
    all_gather x1, waiting for transfers between devices, local(): lax.all_gather(out_weight[0], ('xl', 'zl', 'dp'), axis=0, tiled=True)  102 us
    reduce_scatter x1, waiting for transfers between devices, local(): lax.psum_scatter(spread.astype(jnp.bfloat16), ('xl', 'zl'), scatter_dimen...  83.3 us
    psum x1, waiting for transfers between devices, local(): lax.psum(grad_down[owners - 2 * half:].astype(jnp.bfloat16), ('xl', 'zl'))  79.8 us
    all_gather x1, waiting for transfers between devices, local(): lax.all_gather(pair_shard(shard[:, :half], shard[:, half:], is_low, 2), (...  73.8 us
    ppermute x1, waiting for transfers between devices, local(): other = lax.ppermute(source, ('xh', 'sec'), pairs)  17.4 us
  transfers between devices with their start and end apart: 12, of which 9 were waited for; matrix products, arithmetic and copies ran while one was open for 8% of the time, Pallas kernels for 0%

profile of v1, /device:TPU:1, one launch (start us, length us, event | category | flops | bytes accessed | tf_op | source)
XLA Modules:
  0.0 842.3 jit_solution(16667933280861583742)
XLA Ops:
  8.0 1.1 reshape_squeeze.6
  10.0 3.6 collective-permute-start.3
  13.6 4.4 collective-permute-done.3
  18.1 0.8 pad_maximum_fusion.2
  19.1 3.8 collective-permute-start.1
  22.9 3.3 collective-permute-done.1
  26.3 0.9 pad_maximum_fusion.3
  27.3 7.0 collective-permute-start.2
  34.4 17.4 %collective-permute-done.2 = bf16[256,1536]{1,0:T(8,128)(2,1)S(1)} collective-permute-done((bf16[256,1536]{1,0:T(8,128)(2,1)S(1)}, bf16[256,1536]{1,0:T(8,128)(2,1)S(1)}, u32[]{:S(2)}, u32[]{:S(2)}) %collective-permute-start.2) | collective-permute-done | bytes 786464 | tf_op jit(solution)/shard_map/ppermute | solution.py:92
  51.9 0.9 copy-done.7
  52.8 0.7 copy.174
  53.7 358.4 %all-gather.7.cloned.1.call-done = bf16[1536,2432]{1,0:T(8,128)(2,1)} async-done(((bf16[96,2432]{1,0:T(8,128)(2,1)}), bf16[1536,2432]{1,0:T(8,128)(2,1)}) %all-gather.7.cloned.1.call-update) | async-done | bytes 7471120 | tf_op jit(solution)/shard_map/all_gather | solution.py:74
  412.1 6.8 fusion.47
  418.9 1.9 fusion.44
  421.1 1.9 copy.184
  423.5 1.6 copy.182
  425.2 73.8 %all-gather.5.cloned.1.call-done = bf16[3,3,768,256]{3,2,1,0:T(8,128)(2,1)} async-done(((bf16[3,3,96,256]{3,2,1,0:T(8,128)(2,1)}), bf16[3,3,768,256]{3,2,1,0:T(8,128)(2,1)}) %all-gather.5.cloned.1.call-update) | async-done | bytes 3538960 | tf_op jit(solution)/shard_map/all_gather | solution.py:79
  499.0 2.5 fusion.26
  501.5 1.1 fusion.24
  502.9 1.9 negate_convert_fusion
  504.8 0.9 fusion.23
  505.8 4.6 fusion.17
  510.4 5.3 fusion.16
  515.7 1.9 pad_maximum_fusion
  518.0 0.9 copy-done.6
  518.9 0.8 slice.126
  520.6 4.5 fusion.25
  525.1 5.7 fusion.11
  530.8 1.1 fusion.12
  531.9 101.6 %all-gather.9.cloned.1.call-done = bf16[1,768,1536]{2,1,0:T(8,128)(2,1)} async-done(((bf16[1,48,1536]{2,1,0:T(8,128)(2,1)}), bf16[1,768,1536]{2,1,0:T(8,128)(2,1)}) %all-gather.9.cloned.1.call-update) | async-done | bytes 2359312 | tf_op jit(solution)/shard_map/all_gather | solution.py:82
  633.5 3.3 fusion.3
  636.8 1.0 slice.169
  637.8 5.4 collective-permute-start.4
  643.2 83.3 %reduce-scatter.2.cloned.1.call-done = bf16[1,768,256]{2,1,0:T(8,128)(2,1)} async-done(((bf16[8,768,256]{2,1,0:T(8,128)(2,1)}), bf16[1,768,256]{2,1,0:T(8,128)(2,1)}) %reduce-scatter.2.cloned.1.call-update) | async-done | bytes 393232 | tf_op jit(solution)/shard_map/reduce_scatter | solution.py:128
  726.5 1.8 constant_dynamic-update-slice_fusion.1
  728.2 79.8 %all-reduce.3.cloned.1.call-done = bf16[1,768,256]{2,1,0:T(8,128)(2,1)} async-done(((bf16[1,768,256]{2,1,0:T(8,128)(2,1)}), bf16[1,768,256]{2,1,0:T(8,128)(2,1)}) %all-reduce.3.cloned.1.call-update) | async-done | bytes 393232 | tf_op jit(solution)/shard_map/psum | solution.py:127
  808.1 1.8 constant_dynamic-update-slice_fusion
  809.8 1.9 select_reduce_fusion
  811.8 0.8 fusion.22
  814.0 0.7 fusion.21
  815.4 1.6 fusion.18
  817.7 2.3 collective-permute-start.5
  820.0 0.8 copy.194
  820.8 3.6 all-to-all-start
  824.4 2.5 fusion.32
  826.9 0.8 bitcast_select_fusion.2
  827.7 6.4 all-to-all-done
  834.7 1.1 subtract_multiply_fusion
  (77 shorter events, 8.2 us)
Async XLA Ops:
  7.2 404.9 %all-gather.7.cloned.1.call-start = ((), (), s32[]{:S(2)}) async-start(), calls=%async_computation.3 | async-start | bytes 7938048 | tf_op jit(solution)/shard_map/all_gather | solution.py:74
  9.9 9.1 %copy-start.1 = (f32[1,1,3,6,48,256]{5,4,3,2,1,0:T(8,128)S(1)}, f32[1,1,3,6,48,256]{5,4,3,2,1,0:T(8,128)}, u32[]{:S(2)}) copy-start(f32[1,1,3,6,48,256]{5,4,3,2,1,0:T(8,128)} %param.11) | copy-start | bytes 2654212
  10.0 8.0 collective-permute-start.3
  18.9 480.1 %all-gather.5.cloned.1.call-start = ((), (), s32[]{:S(2)}) async-start(), calls=%async_computation.2 | async-start | bytes 3981312 | tf_op jit(solution)/shard_map/all_gather | solution.py:79
  19.0 8.2 copy-start.8
  19.1 8.2 copy-start.9
  19.1 7.1 collective-permute-start.1
  27.2 606.3 %all-gather.9.cloned.1.call-start = ((), (), s32[]{:S(2)}) async-start(), calls=%async_computation.6 | async-start | bytes 2506752 | tf_op jit(solution)/shard_map/all_gather | solution.py:82
  27.3 24.5 %collective-permute-start.2 = (bf16[256,1536]{1,0:T(8,128)(2,1)S(1)}, bf16[256,1536]{1,0:T(8,128)(2,1)S(1)}, u32[]{:S(2)}, u32[]{:S(2)}) collective-permute-start(bf16[256,1536]{1,0:T(8,128)(2,1)S(1)} %bitcast_select_fusion), channel_id=1, source_target_pairs={{0,130},{2,132},{4,134},{6,136},{8,138},{10,140},{12,142},{14,128}... | collective-permute-start | bytes 2359304 | tf_op jit(solution)/shard_map/ppermute | solution.py:92
  34.3 17.5 %collective-permute-start = (bf16[256,1536]{1,0:T(8,128)(2,1)S(1)}, bf16[256,1536]{1,0:T(8,128)(2,1)S(1)}, u32[]{:S(2)}, u32[]{:S(2)}) collective-permute-start(bf16[256,1536]{1,0:T(8,128)(2,1)S(1)} %bitcast_select_fusion), channel_id=1, source_target_pairs={{0,2},{2,4},{4,6},{6,8},{8,10},{10,12},{12,14},{14,0},{1,3},{3,5},... | collective-permute-start | bytes 2359304 | tf_op jit(solution)/shard_map/ppermute | solution.py:86
  34.4 692.1 %reduce-scatter.2.cloned.1.call-start = ((), (), s32[]{:S(2)}) async-start(), calls=%async_computation.4 | async-start | bytes 3538944 | tf_op jit(solution)/shard_map/reduce_scatter | solution.py:128
  51.9 0.9 copy-start.7
  499.0 2.5 copy-start.11
  501.5 1.4 copy-start.4
  502.6 2.2 copy-start.12
  504.8 1.0 copy-start.5
  510.4 5.3 slice-start
  517.6 1.3 copy-start.6
  517.6 2.1 copy-start.3
  517.7 290.4 %all-reduce.3.cloned.1.call-start = ((), (), s32[]{:S(2)}) async-start(), calls=%async_computation.5 | async-start | bytes 786432 | tf_op jit(solution)/shard_map/psum | solution.py:127
  637.8 186.6 %collective-permute-start.4 = (bf16[256,1536]{1,0:T(8,128)(2,1)}, bf16[256,1536]{1,0:T(8,128)(2,1)}, u32[]{:S(2)}, u32[]{:S(2)}) collective-permute-start(bf16[256,1536]{1,0:T(8,128)(2,1)} %slice.169), channel_id=1, source_target_pairs={{0,128},{128,0},{1,129},{129,1},{2,130},{130,2},{3,131},{131,3},{4... | collective-permute-start | bytes 2359304 | tf_op jit(solution)/shard_map/ppermute | solution.py:27
  814.0 1.4 copy-start
  817.0 3.8 copy-start.10
  817.7 9.2 %collective-permute-start.5 = (bf16[1,48,256]{2,1,0:T(8,128)(2,1)}, bf16[1,48,256]{2,1,0:T(8,128)(2,1)}, u32[]{:S(2)}, u32[]{:S(2)}) collective-permute-start(bf16[1,48,256]{2,1,0:T(8,128)(2,1)} %select_bitcast_fusion), channel_id=1, source_target_pairs={{0,128},{128,0},{1,129},{129,1},{2,130},{130,2},{3,131},{131,3},{4... | collective-permute-start | bytes 73736 | tf_op jit(solution)/shard_map/ppermute | solution.py:27
  820.8 13.3 %all-to-all-start = ((bf16[16,48,256]{2,1,0:T(8,128)(2,1)}), bf16[16,48,256]{2,1,0:T(8,128)(2,1)S(1)}, u32[]{:S(2)}, u32[]{:S(2)}) async-start(bf16[16,48,256]{2,1,0:T(8,128)(2,1)} %bitcast.20), calls=%async_computation.1 | async-start | bytes 786432 | tf_op jit(solution)/shard_map/all_to_all | solution.py:136
  827.7 6.5 copy-start.2
Sparse Core Ops, SparseCore 0:
  19.0 392.9 all-gather.6
  413.9 85.1 all-gather.4
  500.8 132.6 all-gather.8
  635.9 90.5 reduce-scatter.1
  728.9 79.0 all-reduce.2

commit v2 on v1

v2 whole, which is shorter than its diff:
```python
import jax
import jax.numpy as jnp
from jax import lax
from jax.sharding import Mesh
from jax.sharding import PartitionSpec as P

CTX = ("xh", "xl", "zl")
CTX_DP = CTX + ("dp",)
SEC = ("y", "c")
LANES = 128

linear_coef = 3.4445
cubic_coef = -4.775
quintic_coef = 2.0315
update_scale = 8.0
highest = lax.Precision.HIGHEST


def swish(values):
    return values * jax.nn.sigmoid(values)


def unit_rows(values):
    return values / jnp.sqrt(jnp.sum(values * values, axis=-1, keepdims=True) + 1e-06)


def swap_axis(block, axis):
    return lax.ppermute(block, axis, [(0, 1), (1, 0)])


def exchange(block, across):
    route = [
        (4 * x + 2 * a + b, 4 * (x ^ across) + 2 * b + a)
        for x in (0, 1)
        for a in (0, 1)
        for b in (0, 1)
    ]
    return lax.ppermute(block, ("xh", "xl", "c"), route)


def from_section_behind(block, across):
    ys = lax.axis_size("y")
    at = lambda x, a, y, b: ((2 * x + a) * ys + y) * 2 + b
    route = []
    for x in (0, 1):
        for layer in (0, 1):
            for y in range(ys):
                for k in (0, 1):
                    behind = (2 * y + layer - 1) % (2 * ys)
                    source = at(x ^ across, k, behind // 2, behind % 2)
                    route.append((source, at(x, layer, y, k)))
    return lax.ppermute(block, ("xh", "xl", "y", "c"), route)


def pair_shard(low, high, is_low, dim):
    kept = exchange(jnp.where(is_low, low, high), 0)
    got = exchange(jnp.where(is_low, high, low), 1)
    return jnp.concatenate([jnp.where(is_low, kept, got), jnp.where(is_low, got, kept)], axis=dim)


def polynomial(square):
    return (
        linear_coef * jnp.eye(square.shape[-1], dtype=jnp.float32)
        + cubic_coef * square
        + quintic_coef * jnp.dot(square, square, precision=highest)
    )


def orthogonalize(gradient, rows):
    square = jnp.einsum("rd,re->de", gradient, gradient, precision=highest)
    inverse_norm = lax.rsqrt(jnp.trace(square) + 1e-06)
    square = square * inverse_norm * inverse_norm
    first = polynomial(square)
    square = jnp.dot(first, jnp.dot(square, first, precision=highest), precision=highest)
    both = jnp.dot(first, polynomial(square), precision=highest)
    return jnp.dot(rows * inverse_norm, both, precision=highest).astype(jnp.bfloat16)


def local(fresh_input, carried, qkv_weight, out_weight, rate_weight, fast_state):
    is_low = lax.axis_index("xh") == 0
    core = lax.axis_index("c")
    is_first = core == 0
    heads = rate_weight.shape[2]
    head_dim = fast_state.shape[5]
    half = heads // 2
    width = half * head_dim
    rows = qkv_weight.shape[1]
    count, channels = fresh_input.shape[1:]
    dots = lambda a, b: jnp.dot(a, b, preferred_element_type=jnp.float32)

    w = qkv_weight[0]
    part = lambda i, h: w[:, (2 * i + h) * width : (2 * i + h + 1) * width]
    rate = lambda h: jnp.pad(
        rate_weight[0][:, h * half : (h + 1) * half], ((0, 0), (0, LANES - half))
    )
    low, high = (jnp.concatenate([part(1, h), part(2, h), rate(h)], axis=1) for h in (0, 1))
    ring = ("dp", "zl")
    my_kv = lax.all_gather(pair_shard(low, high, is_low, 0), ring, axis=0, tiled=True)

    previous = fast_state[0, 0]
    shard = previous.astype(jnp.bfloat16)
    my_fast = lax.all_gather(
        pair_shard(shard[:, :half], shard[:, half:], is_low, 2), "zl", axis=2, tiled=True
    )

    is_last = lax.axis_index(SEC) == lax.axis_size(SEC) - 1
    source = jnp.where(is_last, fresh_input[0], carried[0, 0])
    mine = from_section_behind(source, 0)
    other = from_section_behind(source, 1)
    inputs = jnp.concatenate([mine, other], axis=0)

    my_q = lax.all_gather(
        pair_shard(part(0, 0), part(0, 1), is_low, 0), ring, axis=0, tiled=True
    )
    my_out = lax.all_gather(exchange(out_weight[0], 0), ring, axis=0, tiled=True)

    zs = lax.axis_size("zl")
    ordered = inputs.reshape(2 * count, 2, 2, zs, -1, rows).transpose(2, 0, 4, 3, 1, 5)
    ordered = ordered.reshape(2, 2 * count, channels // 2)
    my_columns = jnp.where(is_first, ordered[0], ordered[1])
    its_columns = jnp.where(is_first, ordered[1], ordered[0])

    its_kv = swap_axis(my_kv, "c")
    projected = dots(my_columns, my_kv) + dots(its_columns, its_kv)
    by_head = lambda a: a.reshape(2 * count, half, head_dim)
    key_rows = unit_rows(swish(by_head(projected[:, :width]))).astype(jnp.bfloat16)
    value_rows = by_head(projected[:, width : 2 * width]).astype(jnp.bfloat16)
    rates = jax.nn.softplus(projected[:, 2 * width : 2 * width + half])

    its_fast = swap_axis(my_fast, "c")
    fast = jnp.concatenate(
        [jnp.where(is_first, my_fast, its_fast), jnp.where(is_first, its_fast, my_fast)], axis=2
    )
    gate_fast, up_fast, down_fast = (fast[0], fast[1], fast[2])

    gate_pre = jnp.einsum("thd,hfd->htf", key_rows, gate_fast, preferred_element_type=jnp.float32)
    up_pre = jnp.einsum("thd,hfd->htf", key_rows, up_fast, preferred_element_type=jnp.float32)
    sigma = jax.nn.sigmoid(gate_pre)
    gate_act = gate_pre * sigma
    key_hidden = (gate_act * up_pre).astype(jnp.bfloat16)
    scaled_values = (rates[:, :, None] * value_rows.astype(jnp.float32)).astype(jnp.bfloat16)
    hidden_grad = -jnp.einsum(
        "thd,hfd->htf", scaled_values, down_fast, preferred_element_type=jnp.float32
    )
    up_grad = (hidden_grad * gate_act).astype(jnp.bfloat16)
    gate_grad = (hidden_grad * up_pre * sigma * (1.0 + gate_pre * (1.0 - sigma))).astype(
        jnp.bfloat16
    )
    grad_gate = jnp.einsum("htf,thd->hfd", gate_grad, key_rows, preferred_element_type=jnp.float32)
    grad_up = jnp.einsum("htf,thd->hfd", up_grad, key_rows, preferred_element_type=jnp.float32)
    grad_down = -jnp.einsum(
        "htf,thd->hfd", key_hidden, scaled_values, preferred_element_type=jnp.float32
    )

    hidden_units = fast.shape[2]
    owners = 2 * zs
    grads = [a.astype(jnp.bfloat16) for a in (grad_gate, grad_up, grad_down)]
    whole = jnp.concatenate([grads[0], grads[1], grads[2][: owners - 2 * half]], axis=0)
    ninth = grads[2][owners - 2 * half :].reshape(owners, hidden_units // owners, head_dim)
    spread = jnp.concatenate([whole, ninth], axis=1)
    kept = jnp.where(is_first, spread[:zs], spread[zs:])
    got = swap_axis(jnp.where(is_first, spread[zs:], spread[:zs]), "c")
    summed = (kept.astype(jnp.float32) + got.astype(jnp.float32)).astype(jnp.bfloat16)
    parts = lax.all_to_all(summed, "zl", 0, 0, tiled=True)
    owned = jnp.sum(parts.astype(jnp.float32), axis=0)
    own, own_rows = owned[:hidden_units], owned[hidden_units:]
    small = own_rows.astype(jnp.bfloat16)
    small = jnp.concatenate([small, swap_axis(small, "c")], axis=0)
    small = lax.all_to_all(jnp.broadcast_to(small[None], (zs,) + small.shape), "zl", 0, 0, tiled=True)
    small = small.reshape(hidden_units, head_dim).astype(jnp.float32)

    shard_rows = previous.shape[2]
    current = orthogonalize(own, own).reshape(owners, 2, shard_rows, head_dim)
    outgoing = current.transpose(1, 0, 2, 3).reshape(2 * owners, shard_rows, head_dim)
    arrived = lax.all_to_all(outgoing, ("xh", "c", "zl"), 0, 0, tiled=True)
    arrived = arrived.reshape(2, owners, shard_rows, head_dim)
    last = orthogonalize(small, own_rows).reshape(2, shard_rows, head_dim)
    kept = jnp.where(is_low, last[0], last[1])
    got = swap_axis(jnp.where(is_low, last[1], last[0]), "xh")
    last = jnp.stack([jnp.where(is_low, kept, got), jnp.where(is_low, got, kept)])
    current = exchange(jnp.concatenate([arrived, last[:, None]], axis=1), 0).astype(jnp.float32)
    current = current.reshape(2, 3, half, shard_rows, head_dim).transpose(1, 0, 2, 3, 4)
    current = current.reshape(previous.shape)
    stepped = previous - update_scale * current
    rescale = jnp.sqrt(jnp.mean(previous * previous, axis=-1, keepdims=True) + 1e-06) * lax.rsqrt(
        jnp.mean(stepped * stepped, axis=-1, keepdims=True) + 1e-06
    )
    new_state = (stepped * rescale)[None, None]

    query = dots(my_columns, my_q) + dots(its_columns, swap_axis(my_q, "c"))
    query_rows = unit_rows(swish(by_head(query))).astype(jnp.bfloat16)
    gate_query = jnp.einsum(
        "thd,hfd->htf", query_rows, gate_fast, preferred_element_type=jnp.float32
    )
    up_query = jnp.einsum("thd,hfd->htf", query_rows, up_fast, preferred_element_type=jnp.float32)
    hidden = (swish(gate_query) * up_query).astype(jnp.bfloat16)
    mixture = jnp.einsum("htf,hfd->thd", hidden, down_fast, preferred_element_type=jnp.float32)
    head_out = (
        mixture * lax.rsqrt(jnp.mean(mixture * mixture, axis=-1, keepdims=True) + 1e-05)
    ).astype(jnp.bfloat16)
    ordered = head_out.reshape(2 * count, 2, zs, -1, rows).transpose(1, 0, 3, 2, 4)
    ordered = ordered.reshape(2, 2 * count, width // 2)
    branch_out = dots(jnp.where(is_first, ordered[0], ordered[1]), my_out) + dots(
        jnp.where(is_first, ordered[1], ordered[0]), swap_axis(my_out, "c")
    )
    from_pair = swap_axis(branch_out[count:].astype(jnp.bfloat16), "xh")
    passed = (
        mine.astype(jnp.float32) + (branch_out[:count] + from_pair.astype(jnp.float32))
    ).astype(jnp.bfloat16)
    passed = exchange(passed, 0)
    return (passed[None, None], new_state)


def solution(mesh):
    shape = (2, 2, 4, mesh.shape["sec"] // 2, 2, mesh.shape["dp"])
    split = Mesh(mesh.devices.reshape(shape), ("xh", "xl", "zl", "y", "c", "dp"))
    in_specs = (
        P("dp", CTX, None),
        P(SEC, "dp", CTX, None),
        P(SEC, CTX_DP, None),
        P(SEC, CTX_DP, None),
        P(SEC, CTX_DP, None),
        P(SEC, "dp", None, None, CTX, None),
    )
    out_specs = (P(SEC, "dp", CTX, None), P(SEC, "dp", None, None, CTX, None))
    return jax.shard_map(local, mesh=split, in_specs=in_specs, out_specs=out_specs, check_vma=False)
```

time: 849 us -> 387 us (0.46)
  waiting for transfers between devices: 728 us -> 186 us
  starting transfers between devices: 26.1 us -> 61 us
  matrix products: 43.6 us -> 69.3 us
  other arithmetic: 12 us -> 27.4 us
    all_gather x3 -> x4, waiting for transfers between devices: 534 us -> 90.4 us  [the longest x1 43.8 us: local(): lax.all_gather(pair_shard(shard[:, :half], shard[:, half:], is_low, 2), '...]
    reduce_scatter x1 -> x0, waiting for transfers between devices: 83.3 us -> none  [local(): lax.psum_scatter(spread.astype(jnp.bfloat16), ('xl', 'zl'), scatter_dimen...]
    psum x1 -> x0, waiting for transfers between devices: 79.8 us -> none  [local(): lax.psum(grad_down[owners - 2 * half:].astype(jnp.bfloat16), ('xl', 'zl'))]
    ppermute x6 -> x19, waiting for transfers between devices: 25.2 us -> 62.2 us  [the longest x2 32.9 us: from_section_behind(): return lax.ppermute(block, ('xh', 'xl', 'y', 'c'), route)]
    all_to_all x1 -> x3, waiting for transfers between devices: 6.35 us -> 33.7 us  [the longest x1 25.5 us: local(): parts = lax.all_to_all(summed, 'zl', 0, 0, tiled=True)]
    ppermute x6 -> x19, starting transfers between devices: 22.1 us -> 45.4 us  [the longest x9 20.8 us: exchange(): return lax.ppermute(block, ('xh', 'xl', 'c'), route)]
    dot_general x9 -> x20, matrix products: 17.2 us -> 30.5 us  [the longest x6 12.8 us: local(): dots = lambda a, b: jnp.dot(a, b, preferred_element_type=jnp.float32)]
    all_to_all x1 -> x3, starting transfers between devices: 3.55 us -> 15.4 us  [the longest x1 6.4 us: local(): arrived = lax.all_to_all(outgoing, ('xh', 'c', 'zl'), 0, 0, tiled=True)]
  transfers between devices with their start and end apart: 12 -> 26, of which waited for: 9 -> 15; matrix products, arithmetic and copies ran while one was open for 8% -> 28% of each run, Pallas kernels for 0% -> 0%
where the time goes in v2:
time: 387 us; the launch traced here: 381 us
  waiting for transfers between devices  186 us (48%)
  matrix products  69.3 us (18%)
  starting transfers between devices  61 us (16%)
  other arithmetic  27.4 us (7%)
  local copies, waits for them, and re-layouts  20.1 us (5%)
  between operations  16.4 us (4%)
    all_gather x1, waiting for transfers between devices, local(): lax.all_gather(pair_shard(shard[:, :half], shard[:, half:], is_low, 2), '...  43.8 us
    ppermute x2, waiting for transfers between devices, from_section_behind(): return lax.ppermute(block, ('xh', 'xl', 'y', 'c'), route)  32.9 us
    ppermute x9, waiting for transfers between devices, exchange(): return lax.ppermute(block, ('xh', 'xl', 'c'), route)  29.3 us
    all_gather x1, waiting for transfers between devices, local(): lax.all_gather(exchange(out_weight[0], 0), ring, axis=0, tiled=True)  29 us
    all_to_all x1, waiting for transfers between devices, local(): parts = lax.all_to_all(summed, 'zl', 0, 0, tiled=True)  25.5 us
    ppermute x9, starting transfers between devices, exchange(): return lax.ppermute(block, ('xh', 'xl', 'c'), route)  20.8 us
    ppermute x8, starting transfers between devices, swap_axis(): return lax.ppermute(block, axis, [(0, 1), (1, 0)])  20.7 us
    all_gather x1, waiting for transfers between devices, local(): lax.all_gather(pair_shard(low, high, is_low, 0), ring, axis=0, tiled=True)  17.6 us
  transfers between devices with their start and end apart: 26, of which 15 were waited for; matrix products, arithmetic and copies ran while one was open for 28% of the time, Pallas kernels for 0%

profile of v2, /device:TPU:1, one launch (start us, length us, event | category | flops | bytes accessed | tf_op | source)
XLA Modules:
  0.0 380.6 jit_solution(16480532736955415451)
XLA Ops:
  9.4 4.5 %collective-permute-start.12 = (bf16[48,1664]{1,0:T(8,128)(2,1)S(1)}, bf16[48,1664]{1,0:T(8,128)(2,1)S(1)}, u32[]{:S(2)}, u32[]{:S(2)}) collective-permute-start(bf16[48,1664]{1,0:T(8,128)(2,1)S(1)} %get-tuple-element.22), channel_id=1, source_target_pairs={{0,0},{2,64},{64,2},{66,66},{128,128},{130,192},{192,130},{194,194... | collective-permute-start | bytes 479240 | tf_op jit(solution)/shard_map/ppermute | solution.py:38
  15.5 3.2 collective-permute-done.12
  18.7 2.7 collective-permute-done.13
  22.4 2.1 collective-permute-start.1
  26.2 3.8 %collective-permute-done.1 = bf16[3,3,48,256]{3,2,1,0:T(8,128)(2,1)S(1)} collective-permute-done((bf16[3,3,48,256]{3,2,1,0:T(8,128)(2,1)S(1)}, bf16[3,3,48,256]{3,2,1,0:T(8,128)(2,1)S(1)}, u32[]{:S(2)}, u32[]{:S(2)}) %collective-permute-start.1) | collective-permute-done | bytes 221216 | tf_op jit(solution)/shard_map/ppermute | solution.py:38
  30.1 2.9 collective-permute-done.2
  37.1 2.9 collective-permute-done.5
  42.1 2.0 collective-permute-start.8
  44.1 17.6 %all-gather.11.cloned.1.call-done = bf16[768,1664]{1,0:T(8,128)(2,1)} async-done(((bf16[96,1664]{1,0:T(8,128)(2,1)}), bf16[768,1664]{1,0:T(8,128)(2,1)}) %all-gather.11.cloned.1.call-update) | async-done | bytes 2555920 | tf_op jit(solution)/shard_map/all_gather | solution.py:98
  61.7 4.1 %collective-permute-start.14 = (bf16[768,1664]{1,0:T(8,128)(2,1)}, bf16[768,1664]{1,0:T(8,128)(2,1)}, u32[]{:S(2)}, u32[]{:S(2)}) collective-permute-start(bf16[768,1664]{1,0:T(8,128)(2,1)} %all-gather.11.cloned.1.call-done), channel_id=1, source_target_pairs={{0,2},{2,0},{1,3},{3,1},{4,6},{6,4},{5,7},{7,5},{8,10},{10,8},{9,1... | collective-permute-start | bytes 7667720 | tf_op jit(solution)/shard_map/ppermute | solution.py:28
  66.5 43.8 %all-gather.5.cloned.1.call-done = bf16[3,3,384,256]{3,2,1,0:T(8,128)(2,1)} async-done(((bf16[3,3,96,256]{3,2,1,0:T(8,128)(2,1)}), bf16[3,3,384,256]{3,2,1,0:T(8,128)(2,1)}) %all-gather.5.cloned.1.call-update) | async-done | bytes 1769488 | tf_op jit(solution)/shard_map/all_gather | solution.py:102
  111.6 3.6 collective-permute-start.4
  115.5 27.3 %collective-permute-done.4 = bf16[256,1536]{1,0:T(8,128)(2,1)S(1)} collective-permute-done((bf16[256,1536]{1,0:T(8,128)(2,1)S(1)}, bf16[256,1536]{1,0:T(8,128)(2,1)S(1)}, u32[]{:S(2)}, u32[]{:S(2)}) %collective-permute-start.4) | collective-permute-done | bytes 786464 | tf_op jit(solution)/shard_map/ppermute | solution.py:52
  143.7 5.5 %collective-permute-done = bf16[256,1536]{1,0:T(8,128)(2,1)S(1)} collective-permute-done((bf16[256,1536]{1,0:T(8,128)(2,1)S(1)}, bf16[256,1536]{1,0:T(8,128)(2,1)S(1)}, u32[]{:S(2)}, u32[]{:S(2)}) %collective-permute-start) | collective-permute-done | bytes 786464 | tf_op jit(solution)/shard_map/ppermute | solution.py:52
  153.3 2.6 collective-permute-start.7
  155.9 29.0 %all-gather.9.cloned.1.call-done = bf16[384,1536]{1,0:T(8,128)(2,1)} async-done(((bf16[48,1536]{1,0:T(8,128)(2,1)}), bf16[384,1536]{1,0:T(8,128)(2,1)}) %all-gather.9.cloned.1.call-update) | async-done | bytes 1179664 | tf_op jit(solution)/shard_map/all_gather | solution.py:115
  184.8 5.9 %collective-permute-start.9 = (bf16[384,1536]{1,0:T(8,128)(2,1)}, bf16[384,1536]{1,0:T(8,128)(2,1)}, u32[]{:S(2)}, u32[]{:S(2)}) collective-permute-start(bf16[384,1536]{1,0:T(8,128)(2,1)} %all-gather.9.cloned.1.call-done), channel_id=1, source_target_pairs={{0,2},{2,0},{1,3},{3,1},{4,6},{6,4},{5,7},{7,5},{8,10},{10,8},{9,1... | collective-permute-start | bytes 3538952 | tf_op jit(solution)/shard_map/ppermute | solution.py:28
  190.7 3.6 broadcast_select_fusion.1
  194.3 3.5 fusion.67
  200.9 3.0 copy.58
  205.8 5.1 %fusion.51 = f32[3,512,768]{2,1,0:T(8,128)} fusion(bf16[3,3,384,256]{3,2,1,0:T(8,128)(2,1)} %get-tuple-element.4, bf16[3,3,384,256]{3,2,1,0:T(8,128)(2,1)} %get-tuple-element.5, f32[512,3]{0,1:T(4,128)S(1)} %add_sqrt_fusion, f32[512,3,256]{0,2,1:T(8,128)} %bitcast.115), kind=kOutput, calls=%fused_computation.137 | convolution fusion | flops 608698368 | bytes 9836544 | tf_op jit(solution)/shard_map/thd,hfd->htf/dot_general | solution.py:137
  210.9 3.3 fusion.57
  216.3 2.0 copy.56
  219.4 2.1 fusion.35
  221.5 4.6 %fusion.12 = bf16[3,768,256]{2,1,0:T(8,128)(2,1)S(1)} fusion(f32[3,512,768]{2,1,0:T(8,128)S(1)} %fusion.35, f32[3,512,768]{2,1,0:T(8,128)} %fusion.57, f32[512,3]{0,1:T(4,128)S(1)} %add_sqrt_fusion, f32[512,3,256]{0,2,1:T(8,128)S(1)} %bitcast.117), kind=kOutput, calls=%fused_computation.42 | convolution fusion | flops 615186432 | bytes 12195840 | tf_op jit(solution)/shard_map/htf,thd->hfd/dot_general | solution.py:150
  226.1 6.8 %fusion.11 = bf16[3,768,256]{2,1,0:T(8,128)(2,1)S(1)} fusion(f32[3,512,768]{2,1,0:T(8,128)} %fusion.57, f32[3,512,768]{2,1,0:T(8,128)} %fusion.51, f32[3,512,768]{2,1,0:T(8,128)S(1)} %fusion.35, f32[512,3]{0,1:T(4,128)S(1)} %add_sqrt_fusion, f32[512,3,256]{0,2,1:T(8,128)S(1)} %bitcast.118), kind=kOutput, calls=%fused_computation.41 | convolution fusion | flops 619905024 | bytes 16914432 | tf_op jit(solution)/shard_map/htf,thd->hfd/dot_general | solution.py:149
  232.9 5.5 %negate_convert_fusion = bf16[3,768,256]{2,1,0:T(8,128)(2,1)S(1)} fusion(f32[3,512,768]{2,1,0:T(8,128)} %fusion.51, f32[3,512,768]{2,1,0:T(8,128)} %fusion.57, f32[512,3,256]{0,2,1:T(8,128)S(1)} %bitcast.121, f32[512,3]{0,1:T(4,128)S(1)} %copy.55), kind=kOutput, calls=%fused_computation.17 | convolution fusion | flops 613023744 | bytes 12195840 | tf_op jit(solution)/shard_map/htf,thd->hfd/dot_general | solution.py:151
  240.6 2.2 fusion.65
  242.9 2.0 convolution_add_fusion.2
  244.8 3.0 copy.48
  249.7 4.9 %fusion.59 = f32[3,512,768]{2,1,0:T(8,128)} fusion(bf16[3,3,384,256]{3,2,1,0:T(8,128)(2,1)} %get-tuple-element.5, bf16[3,3,384,256]{3,2,1,0:T(8,128)(2,1)} %get-tuple-element.4, f32[512,3]{0,1:T(4,128)S(1)} %add_sqrt_fusion.1, f32[512,3,256]{0,2,1:T(8,128)} %bitcast.112), kind=kOutput, calls=%fused_computation.139 | convolution fusion | flops 608698368 | bytes 9836544 | tf_op jit(solution)/shard_map/thd,hfd->htf/dot_general | solution.py:192
  254.7 3.4 add_convert_fusion
  258.1 4.9 %all-to-all-start = ((bf16[4,864,256]{2,1,0:T(8,128)(2,1)}), bf16[4,864,256]{2,1,0:T(8,128)(2,1)}, u32[]{:S(2)}, u32[]{:S(2)}) async-start(bf16[4,864,256]{2,1,0:T(8,128)(2,1)} %add_convert_fusion), calls=%async_computation | async-start | bytes 3538944 | tf_op jit(solution)/shard_map/all_to_all | solution.py:164
  263.0 6.5 %fusion.9 = (f32[512,3]{0,1:T(4,128)S(1)}, f32[3,256,512]{2,1,0:T(8,128)}) fusion(f32[3,512,768]{2,1,0:T(8,128)} %fusion.59, bf16[3,3,384,256]{3,2,1,0:T(8,128)(2,1)S(1)} %copy-done.8, bf16[3,3,384,256]{3,2,1,0:T(8,128)(2,1)S(1)} %copy-done.10, f32[512,3]{0,1:T(4,128)S(1)} %add_sqrt_fusion.1, f32[512,3,256]{0,2,1:T(8,128)} %bitcast.113), kind=kOutput, calls=%fused_computation.32 | convolution fusion | flops 1222900224 | bytes 14956544 | tf_op jit(solution)/shard_map/htf,hfd->thd/dot_general | solution.py:197
  271.3 2.4 fusion.66
  275.7 2.7 collective-permute-start.10
  278.4 25.5 %all-to-all-done = bf16[4,864,256]{2,1,0:T(8,128)(2,1)} async-done(((bf16[4,864,256]{2,1,0:T(8,128)(2,1)}), bf16[4,864,256]{2,1,0:T(8,128)(2,1)}, u32[]{:S(2)}, u32[]{:S(2)}) %all-to-all-start) | async-done | bytes 1769504 | tf_op jit(solution)/shard_map/all_to_all | solution.py:164
  306.6 2.8 select_reduce_fusion.1
  316.1 4.1 %all-to-all-start.2 = ((bf16[4,192,256]{2,1,0:T(8,128)(2,1)}), bf16[4,192,256]{2,1,0:T(8,128)(2,1)}, u32[]{:S(2)}, u32[]{:S(2)}) async-start(bf16[4,192,256]{2,1,0:T(8,128)(2,1)} %broadcast_in_dim.13), calls=%async_computation.2 | async-start | bytes 786432 | tf_op jit(solution)/shard_map/all_to_all | solution.py:169
  323.8 8.3 %all-to-all-done.2 = bf16[4,192,256]{2,1,0:T(8,128)(2,1)} async-done(((bf16[4,192,256]{2,1,0:T(8,128)(2,1)}), bf16[4,192,256]{2,1,0:T(8,128)(2,1)}, u32[]{:S(2)}, u32[]{:S(2)}) %all-to-all-start.2) | async-done | bytes 393248 | tf_op jit(solution)/shard_map/all_to_all | solution.py:169
  332.1 6.4 %all-to-all-start.1 = ((bf16[16,48,256]{2,1,0:T(8,128)(2,1)}), bf16[16,48,256]{2,1,0:T(8,128)(2,1)S(1)}, u32[]{:S(2)}, u32[]{:S(2)}) async-start(bf16[16,48,256]{2,1,0:T(8,128)(2,1)} %bitcast.26), calls=%async_computation.1 | async-start | bytes 786432 | tf_op jit(solution)/shard_map/all_to_all | solution.py:175
  338.5 2.8 select_reduce_fusion
  347.5 2.9 collective-permute-start.17
  350.4 2.3 fusion.8
  352.7 2.7 collective-permute-start.11
  355.6 2.9 collective-permute-start.18
  358.6 7.7 %collective-permute-done.11 = bf16[256,1536]{1,0:T(8,128)(2,1)S(1)} collective-permute-done((bf16[256,1536]{1,0:T(8,128)(2,1)}, bf16[256,1536]{1,0:T(8,128)(2,1)S(1)}, u32[]{:S(2)}, u32[]{:S(2)}) %collective-permute-start.11) | collective-permute-done | bytes 786464 | tf_op jit(solution)/shard_map/ppermute | solution.py:38
  366.3 4.7 %collective-permute-done.18 = bf16[2,9,48,256]{3,2,1,0:T(8,128)(2,1)S(1)} collective-permute-done((bf16[2,9,48,256]{3,2,1,0:T(8,128)(2,1)S(1)}, bf16[2,9,48,256]{3,2,1,0:T(8,128)(2,1)S(1)}, u32[]{:S(2)}, u32[]{:S(2)}) %collective-permute-start.18) | collective-permute-done | bytes 442400 | tf_op jit(solution)/shard_map/ppermute | solution.py:38
  (145 shorter events, 55.9 us)
Async XLA Ops:
  7.2 15.1 %copy-start = (f32[1,1,3,6,48,256]{5,4,3,2,1,0:T(8,128)S(1)}, f32[1,1,3,6,48,256]{5,4,3,2,1,0:T(8,128)}, u32[]{:S(2)}) copy-start(f32[1,1,3,6,48,256]{5,4,3,2,1,0:T(8,128)} %param.11) | copy-start | bytes 2654212
  7.2 54.5 %all-gather.11.cloned.1.call-start = ((), (), s32[]{:S(2)}) async-start(), calls=%async_computation.6 | async-start | bytes 2875392 | tf_op jit(solution)/shard_map/all_gather | solution.py:98
  9.4 9.3 %collective-permute-start.12 = (bf16[48,1664]{1,0:T(8,128)(2,1)S(1)}, bf16[48,1664]{1,0:T(8,128)(2,1)S(1)}, u32[]{:S(2)}, u32[]{:S(2)}) collective-permute-start(bf16[48,1664]{1,0:T(8,128)(2,1)S(1)} %get-tuple-element.22), channel_id=1, source_target_pairs={{0,0},{2,64},{64,2},{66,66},{128,128},{130,192},{192,130},{194,194... | collective-permute-start | bytes 479240 | tf_op jit(solution)/shard_map/ppermute | solution.py:38
  13.9 7.5 %collective-permute-start.13 = (bf16[48,1664]{1,0:T(8,128)(2,1)S(1)}, bf16[48,1664]{1,0:T(8,128)(2,1)S(1)}, u32[]{:S(2)}, u32[]{:S(2)}) collective-permute-start(bf16[48,1664]{1,0:T(8,128)(2,1)S(1)} %get-tuple-element.23), channel_id=1, source_target_pairs={{0,128},{2,192},{64,130},{66,194},{128,0},{130,64},{192,2},{194,66... | collective-permute-start | bytes 479240 | tf_op jit(solution)/shard_map/ppermute | solution.py:38
  22.2 88.2 %all-gather.5.cloned.1.call-start = ((), (), s32[]{:S(2)}) async-start(), calls=%async_computation.3 | async-start | bytes 2211840 | tf_op jit(solution)/shard_map/all_gather | solution.py:102
  22.3 19.8 %copy-start.25 = (bf16[1,48,1536]{2,1,0:T(8,128)(2,1)S(1)}, bf16[1,48,1536]{2,1,0:T(8,128)(2,1)}, u32[]{:S(2)}) copy-start(bf16[1,48,1536]{2,1,0:T(8,128)(2,1)} %param.9) | copy-start | bytes 442372
  22.4 89.2 %copy-start.21 = (bf16[1,1,256,1536]{3,2,1,0:T(8,128)(2,1)S(1)}, bf16[1,1,256,1536]{3,2,1,0:T(8,128)(2,1)}, u32[]{:S(2)}) copy-start(bf16[1,1,256,1536]{3,2,1,0:T(8,128)(2,1)} %param.7) | copy-start | bytes 2359300
  22.4 89.2 %copy-start.22 = (bf16[1,256,1536]{2,1,0:T(8,128)(2,1)S(1)}, bf16[1,256,1536]{2,1,0:T(8,128)(2,1)}, u32[]{:S(2)}) copy-start(bf16[1,256,1536]{2,1,0:T(8,128)(2,1)} %param.6) | copy-start | bytes 2359300
  22.4 7.7 %collective-permute-start.1 = (bf16[3,3,48,256]{3,2,1,0:T(8,128)(2,1)S(1)}, bf16[3,3,48,256]{3,2,1,0:T(8,128)(2,1)S(1)}, u32[]{:S(2)}, u32[]{:S(2)}) collective-permute-start(bf16[3,3,48,256]{3,2,1,0:T(8,128)(2,1)S(1)} %get-tuple-element.18), channel_id=1, source_target_pairs={{0,0},{2,64},{64,2},{66,66},{128,128},{130,192},{192,130},{194,194... | collective-permute-start | bytes 663560 | tf_op jit(solution)/shard_map/ppermute | solution.py:38
  24.4 8.5 %collective-permute-start.2 = (bf16[3,3,48,256]{3,2,1,0:T(8,128)(2,1)S(1)}, bf16[3,3,48,256]{3,2,1,0:T(8,128)(2,1)S(1)}, u32[]{:S(2)}, u32[]{:S(2)}) collective-permute-start(bf16[3,3,48,256]{3,2,1,0:T(8,128)(2,1)S(1)} %get-tuple-element.19), channel_id=1, source_target_pairs={{0,128},{2,192},{64,130},{66,194},{128,0},{130,64},{192,2},{194,66... | collective-permute-start | bytes 663560 | tf_op jit(solution)/shard_map/ppermute | solution.py:38
  33.9 119.4 %all-gather.7.cloned.1.call-start = ((), (), s32[]{:S(2)}) async-start(), calls=%async_computation.4 | async-start | bytes 1327104 | tf_op jit(solution)/shard_map/all_gather | solution.py:112
  33.9 6.1 %collective-permute-start.5 = (bf16[48,768]{1,0:T(8,128)(2,1)S(1)}, bf16[48,768]{1,0:T(8,128)(2,1)S(1)}, u32[]{:S(2)}, u32[]{:S(2)}) collective-permute-start(bf16[48,768]{1,0:T(8,128)(2,1)S(1)} %get-tuple-element.14), channel_id=1, source_target_pairs={{0,0},{2,64},{64,2},{66,66},{128,128},{130,192},{192,130},{194,194... | collective-permute-start | bytes 221192 | tf_op jit(solution)/shard_map/ppermute | solution.py:38
  35.8 5.5 %collective-permute-start.6 = (bf16[48,768]{1,0:T(8,128)(2,1)S(1)}, bf16[48,768]{1,0:T(8,128)(2,1)S(1)}, u32[]{:S(2)}, u32[]{:S(2)}) collective-permute-start(bf16[48,768]{1,0:T(8,128)(2,1)S(1)} %get-tuple-element.15), channel_id=1, source_target_pairs={{0,128},{2,192},{64,130},{66,194},{128,0},{130,64},{192,2},{194,66... | collective-permute-start | bytes 221192 | tf_op jit(solution)/shard_map/ppermute | solution.py:38
  42.0 142.8 %all-gather.9.cloned.1.call-start = ((), (), s32[]{:S(2)}) async-start(), calls=%async_computation.5 | async-start | bytes 1327104 | tf_op jit(solution)/shard_map/all_gather | solution.py:115
  42.1 23.8 %collective-permute-start.8 = (bf16[48,1536]{1,0:T(8,128)(2,1)S(1)}, bf16[48,1536]{1,0:T(8,128)(2,1)S(1)}, u32[]{:S(2)}, u32[]{:S(2)}) collective-permute-start(bf16[48,1536]{1,0:T(8,128)(2,1)S(1)} %bitcast.135), channel_id=1, source_target_pairs={{0,0},{2,64},{64,2},{66,66},{128,128},{130,192},{192,130},{194,194... | collective-permute-start | bytes 442376 | tf_op jit(solution)/shard_map/ppermute | solution.py:38
  61.7 132.6 %collective-permute-start.14 = (bf16[768,1664]{1,0:T(8,128)(2,1)}, bf16[768,1664]{1,0:T(8,128)(2,1)}, u32[]{:S(2)}, u32[]{:S(2)}) collective-permute-start(bf16[768,1664]{1,0:T(8,128)(2,1)} %all-gather.11.cloned.1.call-done), channel_id=1, source_target_pairs={{0,2},{2,0},{1,3},{3,1},{4,6},{6,4},{5,7},{7,5},{8,10},{10,8},{9,1... | collective-permute-start | bytes 7667720 | tf_op jit(solution)/shard_map/ppermute | solution.py:28
  110.4 80.3 %collective-permute-start.3 = (bf16[3,3,384,256]{3,2,1,0:T(8,128)(2,1)}, bf16[3,3,384,256]{3,2,1,0:T(8,128)(2,1)}, u32[]{:S(2)}, u32[]{:S(2)}) collective-permute-start(bf16[3,3,384,256]{3,2,1,0:T(8,128)(2,1)} %all-gather.5.cloned.1.call-done), channel_id=1, source_target_pairs={{0,2},{2,0},{1,3},{3,1},{4,6},{6,4},{5,7},{7,5},{8,10},{10,8},{9,1... | collective-permute-start | bytes 5308424 | tf_op jit(solution)/shard_map/ppermute | solution.py:28
  111.6 31.2 %collective-permute-start.4 = (bf16[256,1536]{1,0:T(8,128)(2,1)S(1)}, bf16[256,1536]{1,0:T(8,128)(2,1)S(1)}, u32[]{:S(2)}, u32[]{:S(2)}) collective-permute-start(bf16[256,1536]{1,0:T(8,128)(2,1)S(1)} %bitcast_select_fusion), channel_id=1, source_target_pairs={{142,0},{206,2},{130,4},{194,6},{134,8},{198,10},{138,12},{202,14}... | collective-permute-start | bytes 2359304 | tf_op jit(solution)/shard_map/ppermute | solution.py:52
  115.2 34.0 %collective-permute-start = (bf16[256,1536]{1,0:T(8,128)(2,1)S(1)}, bf16[256,1536]{1,0:T(8,128)(2,1)S(1)}, u32[]{:S(2)}, u32[]{:S(2)}) collective-permute-start(bf16[256,1536]{1,0:T(8,128)(2,1)S(1)} %bitcast_select_fusion), channel_id=1, source_target_pairs={{14,0},{78,2},{2,4},{66,6},{6,8},{70,10},{10,12},{74,14},{0,64},{6... | collective-permute-start | bytes 2359304 | tf_op jit(solution)/shard_map/ppermute | solution.py:52
  152.2 38.5 %copy-start.18 = (bf16[3,3,384,256]{3,2,1,0:T(8,128)(2,1)S(1)}, bf16[3,3,384,256]{3,2,1,0:T(8,128)(2,1)}, u32[]{:S(2)}) copy-start(bf16[3,3,384,256]{3,2,1,0:T(8,128)(2,1)} %all-gather.5.cloned.1.call-done) | copy-start | bytes 5308420
  152.3 42.0 %copy-start.13 = (bf16[1,512,2,4,2,48]{1,5,4,3,2,0:T(8,128)(2,1)}, bf16[1,512,2,4,2,48]{1,5,4,3,2,0:T(8,128)(2,1)S(1)}, u32[]{:S(2)}) copy-start(bf16[1,512,2,4,2,48]{1,5,4,3,2,0:T(8,128)(2,1)S(1)} %copy.47) | copy-start | bytes 2359300
  153.3 87.4 %collective-permute-start.7 = (bf16[768,768]{1,0:T(8,128)(2,1)}, bf16[768,768]{1,0:T(8,128)(2,1)}, u32[]{:S(2)}, u32[]{:S(2)}) collective-permute-start(bf16[768,768]{1,0:T(8,128)(2,1)} %all-gather.7.cloned.1.call-done), channel_id=1, source_target_pairs={{0,2},{2,0},{1,3},{3,1},{4,6},{6,4},{5,7},{7,5},{8,10},{10,8},{9,1... | collective-permute-start | bytes 3538952 | tf_op jit(solution)/shard_map/ppermute | solution.py:28
  184.8 86.4 %collective-permute-start.9 = (bf16[384,1536]{1,0:T(8,128)(2,1)}, bf16[384,1536]{1,0:T(8,128)(2,1)}, u32[]{:S(2)}, u32[]{:S(2)}) collective-permute-start(bf16[384,1536]{1,0:T(8,128)(2,1)} %all-gather.9.cloned.1.call-done), channel_id=1, source_target_pairs={{0,2},{2,0},{1,3},{3,1},{4,6},{6,4},{5,7},{7,5},{8,10},{10,8},{9,1... | collective-permute-start | bytes 3538952 | tf_op jit(solution)/shard_map/ppermute | solution.py:28
  194.3 3.5 copy-start.4
  194.3 3.5 copy-start.17
  205.8 5.1 %copy-start.6 = (bf16[3,3,384,256]{3,2,1,0:T(8,128)(2,1)S(1)}, bf16[3,3,384,256]{3,2,1,0:T(8,128)(2,1)}, u32[]{:S(2)}) copy-start(bf16[3,3,384,256]{3,2,1,0:T(8,128)(2,1)} %get-tuple-element.4) | copy-start | bytes 5308420
  205.8 5.1 %copy-start.9 = (bf16[3,3,384,256]{3,2,1,0:T(8,128)(2,1)S(1)}, bf16[3,3,384,256]{3,2,1,0:T(8,128)(2,1)}, u32[]{:S(2)}) copy-start(bf16[3,3,384,256]{3,2,1,0:T(8,128)(2,1)} %get-tuple-element.5) | copy-start | bytes 5308420
  205.8 5.1 %copy-start.11 = (f32[512,768]{0,1:T(8,128)S(1)}, f32[512,768]{0,1:T(8,128)}, u32[]{:S(2)}) copy-start(f32[512,768]{0,1:T(8,128)} %copy.58) | copy-start | bytes 4718596
  216.3 3.1 copy-start.7
  219.4 2.1 copy-start.12
  239.1 1.5 copy-start.14
  240.6 2.3 copy-start.5
  240.6 2.3 copy-start.19
  240.6 14.1 %collective-permute-start.15 = (bf16[4,864,256]{2,1,0:T(8,128)(2,1)}, bf16[4,864,256]{2,1,0:T(8,128)(2,1)}, u32[]{:S(2)}, u32[]{:S(2)}) collective-permute-start(bf16[4,864,256]{2,1,0:T(8,128)(2,1)} %broadcast_select_fusion), channel_id=1, source_target_pairs={{0,2},{2,0},{1,3},{3,1},{4,6},{6,4},{5,7},{7,5},{8,10},{10,8},{9,1... | collective-permute-start | bytes 5308424 | tf_op jit(solution)/shard_map/ppermute | solution.py:28
  258.0 4.9 %copy-start.8 = (bf16[3,3,384,256]{3,2,1,0:T(8,128)(2,1)S(1)}, bf16[3,3,384,256]{3,2,1,0:T(8,128)(2,1)}, u32[]{:S(2)}) copy-start(bf16[3,3,384,256]{3,2,1,0:T(8,128)(2,1)} %get-tuple-element.4) | copy-start | bytes 5308420
  258.1 4.9 %copy-start.10 = (bf16[3,3,384,256]{3,2,1,0:T(8,128)(2,1)S(1)}, bf16[3,3,384,256]{3,2,1,0:T(8,128)(2,1)}, u32[]{:S(2)}) copy-start(bf16[3,3,384,256]{3,2,1,0:T(8,128)(2,1)} %get-tuple-element.5) | copy-start | bytes 5308420
  258.1 45.8 %all-to-all-start = ((bf16[4,864,256]{2,1,0:T(8,128)(2,1)}), bf16[4,864,256]{2,1,0:T(8,128)(2,1)}, u32[]{:S(2)}, u32[]{:S(2)}) async-start(bf16[4,864,256]{2,1,0:T(8,128)(2,1)} %add_convert_fusion), calls=%async_computation | async-start | bytes 3538944 | tf_op jit(solution)/shard_map/all_to_all | solution.py:164
  271.3 2.4 copy-start.20
  275.7 74.8 %collective-permute-start.10 = (bf16[256,1536]{1,0:T(8,128)(2,1)}, bf16[256,1536]{1,0:T(8,128)(2,1)}, u32[]{:S(2)}, u32[]{:S(2)}) collective-permute-start(bf16[256,1536]{1,0:T(8,128)(2,1)} %slice.242), channel_id=1, source_target_pairs={{0,128},{128,0},{1,129},{129,1},{2,130},{130,2},{3,131},{131,3},{4... | collective-permute-start | bytes 2359304 | tf_op jit(solution)/shard_map/ppermute | solution.py:28
  309.4 5.9 %collective-permute-start.16 = (bf16[96,256]{1,0:T(8,128)(2,1)S(1)}, bf16[96,256]{1,0:T(8,128)(2,1)S(1)}, u32[]{:S(2)}, u32[]{:S(2)}) collective-permute-start(bf16[96,256]{1,0:T(8,128)(2,1)S(1)} %slice.243), channel_id=1, source_target_pairs={{0,2},{2,0},{1,3},{3,1},{4,6},{6,4},{5,7},{7,5},{8,10},{10,8},{9,1... | collective-permute-start | bytes 147464 | tf_op jit(solution)/shard_map/ppermute | solution.py:28
  316.1 16.0 %all-to-all-start.2 = ((bf16[4,192,256]{2,1,0:T(8,128)(2,1)}), bf16[4,192,256]{2,1,0:T(8,128)(2,1)}, u32[]{:S(2)}, u32[]{:S(2)}) async-start(bf16[4,192,256]{2,1,0:T(8,128)(2,1)} %broadcast_in_dim.13), calls=%async_computation.2 | async-start | bytes 786432 | tf_op jit(solution)/shard_map/all_to_all | solution.py:169
  320.3 2.0 copy-start.3
  332.1 23.5 %all-to-all-start.1 = ((bf16[16,48,256]{2,1,0:T(8,128)(2,1)}), bf16[16,48,256]{2,1,0:T(8,128)(2,1)S(1)}, u32[]{:S(2)}, u32[]{:S(2)}) async-start(bf16[16,48,256]{2,1,0:T(8,128)(2,1)} %bitcast.26), calls=%async_computation.1 | async-start | bytes 786432 | tf_op jit(solution)/shard_map/all_to_all | solution.py:175
  343.7 6.7 %copy-start.16 = (bf16[256,1536]{1,0:T(8,128)(2,1)S(1)}, bf16[256,1536]{1,0:T(8,128)(2,1)}, u32[]{:S(2)}) copy-start(bf16[256,1536]{1,0:T(8,128)(2,1)} %copy-done.15) | copy-start | bytes 2359300
  347.5 8.0 %collective-permute-start.17 = (bf16[48,256]{1,0:T(8,128)(2,1)S(1)}, bf16[48,256]{1,0:T(8,128)(2,1)S(1)}, u32[]{:S(2)}, u32[]{:S(2)}) collective-permute-start(bf16[48,256]{1,0:T(8,128)(2,1)S(1)} %broadcast_select_fusion.19), channel_id=1, source_target_pairs={{0,128},{128,0},{1,129},{129,1},{2,130},{130,2},{3,131},{131,3},{4... | collective-permute-start | bytes 73736 | tf_op jit(solution)/shard_map/ppermute | solution.py:28
  352.7 13.5 %collective-permute-start.11 = (bf16[256,1536]{1,0:T(8,128)(2,1)}, bf16[256,1536]{1,0:T(8,128)(2,1)S(1)}, u32[]{:S(2)}, u32[]{:S(2)}) collective-permute-start(bf16[256,1536]{1,0:T(8,128)(2,1)} %fusion.8), channel_id=1, source_target_pairs={{0,0},{2,64},{64,2},{66,66},{128,128},{130,192},{192,130},{194,194... | collective-permute-start | bytes 2359304 | tf_op jit(solution)/shard_map/ppermute | solution.py:38
  355.6 15.6 %copy-start.1 = (f32[1,1,3,6,48,256]{5,4,3,2,1,0:T(8,128)S(1)}, f32[1,1,3,6,48,256]{5,4,3,2,1,0:T(8,128)}, u32[]{:S(2)}) copy-start(f32[1,1,3,6,48,256]{5,4,3,2,1,0:T(8,128)} %param.11) | copy-start | bytes 2654212
  355.6 15.4 %collective-permute-start.18 = (bf16[2,9,48,256]{3,2,1,0:T(8,128)(2,1)S(1)}, bf16[2,9,48,256]{3,2,1,0:T(8,128)(2,1)S(1)}, u32[]{:S(2)}, u32[]{:S(2)}) collective-permute-start(bf16[2,9,48,256]{3,2,1,0:T(8,128)(2,1)S(1)} %pad_maximum_fusion.4), channel_id=1, source_target_pairs={{0,0},{2,64},{64,2},{66,66},{128,128},{130,192},{192,130},{194,194... | collective-permute-start | bytes 1327112 | tf_op jit(solution)/shard_map/ppermute | solution.py:38
  (4 other events, 3.4 us)
Sparse Core Ops, SparseCore 0:
  22.3 39.3 all-gather.10
  64.1 46.2 all-gather.4
  112.2 34.4 all-gather.6
  148.3 36.5 all-gather.8
